TPU v7x, 32 devices: a whole 2x2x4 slice. The times are simulated.
32 devices in a mesh: dp: 4 (over x, core), seq: 8 (over z, y).
Axes of the slice: x: 2, y: 2, z: 4, core: 2. Of those that a mesh axis runs over, the one named last changes fastest.
Arguments:
- q_raw: bfloat16 [4, 1024, 4096], P('dp', 'seq'), may hold values from -64 to 64
- k_raw: bfloat16 [4, 1024, 4096], P('dp', 'seq'), may hold values from -64 to 64
- values: bfloat16 [4, 1024, 4096], P('dp', 'seq'), may hold values from -6 to 6
- grad_out: bfloat16 [4, 1024, 4096], P('dp', 'seq'), may hold values from -6 to 6
- q_gain: float32 [4096], replicated, may hold values from 0.1 to 1.9
- k_gain: float32 [4096], replicated, may hold values from 0.1 to 1.9
- lengths: int32 [4, 6], P('dp'), may hold values from 1 to 341, 1024 in all within a row
- positions: int32 [4, 3, 1024], P('dp', None, 'seq'), may hold values from 0 to 63
Outputs:
- attended: bfloat16 [4, 1024, 4096], P('dp', 'seq')
- grad_q: bfloat16 [4, 1024, 4096], P('dp', 'seq')
- grad_k: bfloat16 [4, 1024, 4096], P('dp', 'seq')
- grad_v: bfloat16 [4, 1024, 4096], P('dp', 'seq')
- grad_q_gain: float32 [4096], replicated
- grad_k_gain: float32 [4096], replicated
Inputs may be any that keep to these rules, and one draw needn't show every extreme that they name: `lengths`: the clips of a bucket lie end to end and fill its 1024 tokens.
All inputs are finite; a program needn't handle non-finite values.
Results may differ from a plain program's by a relative error of at most 0.012.
The roundings to bfloat16 on the way count: a program that leaves them out, or rounds other values in their place, can miss the bound.
Values may be sent and summed in bfloat16 or wider, within the bound.
A program may use at most 128 MiB of HBM per device.

v0:
```python
import jax
import jax.numpy as jnp
from jax import lax
from jax.sharding import PartitionSpec as P

HEAD_DIM = 128


epsilon = 1e-06


def product(form, left, right):
    return jnp.einsum(form, left, right, preferred_element_type=jnp.float32)


def segment_ids(clip_lengths, tokens):
    boundary = jnp.cumsum(clip_lengths)
    places = jnp.arange(tokens, dtype=jnp.int32)
    return jnp.sum((boundary[None, :] <= places[:, None]).astype(jnp.int32), axis=1)


def rope_tables(position_rows, head_dim):
    half = head_dim // 2
    sixth = head_dim // 6
    first = half - 2 * sixth
    pairs = jnp.arange(half, dtype=jnp.int32)
    section = (pairs >= first).astype(jnp.int32) + (pairs >= first + sixth).astype(jnp.int32)
    begin = jnp.where(section == 0, 0, jnp.where(section == 1, first, first + sixth))
    number = jnp.where(section == 0, first, sixth)
    freqs = 10000.0 ** (-(pairs - begin).astype(jnp.float32) / number.astype(jnp.float32))
    picker = (section[None, :] == jnp.arange(3, dtype=jnp.int32)[:, None]).astype(
        jnp.float32
    ) * freqs[None, :]
    angle = lax.dot_general(
        position_rows.astype(jnp.float32),
        picker,
        (((0,), (0,)), ((), ())),
        precision=lax.Precision.HIGHEST,
    )
    cosine = jnp.cos(angle)
    sine = jnp.sin(angle)
    return (jnp.concatenate([cosine, cosine], axis=-1), jnp.concatenate([sine, sine], axis=-1))


def rotate_pairs(inputs, cosine, sine):
    half = inputs.shape[-1] // 2
    partner = jnp.concatenate([-inputs[..., half:], inputs[..., :half]], axis=-1)
    return inputs * cosine[:, None, :] + partner * sine[:, None, :]


def rotate_back(grads, cosine, sine):
    half = grads.shape[-1] // 2
    turned = grads * sine[:, None, :]
    return grads * cosine[:, None, :] + jnp.concatenate(
        [turned[..., half:], -turned[..., :half]], axis=-1
    )


def attention_forward(query, keys, value_rows, segment, block, window, reach):
    count = query.shape[0]
    scale = query.shape[2] ** (-0.5)

    def one_block(index_block):
        start = index_block * block
        key_start = jnp.clip(start - reach, 0, count - window)
        query_block = lax.dynamic_slice_in_dim(query, start, block, 0)
        key_window = lax.dynamic_slice_in_dim(keys, key_start, window, 0)
        value_window = lax.dynamic_slice_in_dim(value_rows, key_start, window, 0)
        query_clip = lax.dynamic_slice_in_dim(segment, start, block, 0)
        key_clip = lax.dynamic_slice_in_dim(segment, key_start, window, 0)
        scores = product("qhd,khd->hqk", query_block, key_window) * scale
        live = (query_clip[:, None] == key_clip[None, :])[None]
        scores = jnp.where(live, scores, -1e30)
        highest = jnp.max(scores, axis=-1, keepdims=True)
        expon = jnp.exp(scores - highest)
        totals = jnp.sum(expon, axis=-1, keepdims=True)
        weights = (expon / totals).astype(jnp.bfloat16)
        output = product("hqk,khd->qhd", weights, value_window)
        return (output, (highest + jnp.log(totals))[..., 0])

    outputs, logsum = lax.map(one_block, jnp.arange(count // block, dtype=jnp.int32))
    return (outputs.reshape(query.shape), logsum)


def attention_backward(
    query, keys, value_rows, context, cotangent, logsum, segment, block, window, reach
):
    count = query.shape[0]
    scale = query.shape[2] ** (-0.5)
    delta = jnp.sum(cotangent.astype(jnp.float32) * context.astype(jnp.float32), axis=-1)

    def one_block(carry, inputs):
        key_acc, value_acc = carry
        index_block, block_logsum = inputs
        start = index_block * block
        key_start = jnp.clip(start - reach, 0, count - window)
        query_block = lax.dynamic_slice_in_dim(query, start, block, 0)
        cot_block = lax.dynamic_slice_in_dim(cotangent, start, block, 0)
        delta_block = lax.dynamic_slice_in_dim(delta, start, block, 0)
        key_window = lax.dynamic_slice_in_dim(keys, key_start, window, 0)
        value_window = lax.dynamic_slice_in_dim(value_rows, key_start, window, 0)
        query_clip = lax.dynamic_slice_in_dim(segment, start, block, 0)
        key_clip = lax.dynamic_slice_in_dim(segment, key_start, window, 0)
        scores = product("qhd,khd->hqk", query_block, key_window) * scale
        live = (query_clip[:, None] == key_clip[None, :])[None]
        probs = jnp.where(live, jnp.exp(scores - block_logsum[:, :, None]), 0.0)
        prob_half = probs.astype(jnp.bfloat16)
        value_grad = product("hqk,qhd->khd", prob_half, cot_block)
        dprob = product("qhd,khd->hqk", cot_block, value_window)
        dscore = (probs * (dprob - jnp.transpose(delta_block)[:, :, None]) * scale).astype(
            jnp.bfloat16
        )
        query_grad = product("hqk,khd->qhd", dscore, key_window)
        key_grad = product("hqk,qhd->khd", dscore, query_block)
        key_acc = lax.dynamic_update_slice_in_dim(
            key_acc,
            lax.dynamic_slice_in_dim(key_acc, key_start, window, 0) + key_grad,
            key_start,
            0,
        )
        value_acc = lax.dynamic_update_slice_in_dim(
            value_acc,
            lax.dynamic_slice_in_dim(value_acc, key_start, window, 0) + value_grad,
            key_start,
            0,
        )
        return ((key_acc, value_acc), query_grad)

    zeros = jnp.zeros(query.shape, jnp.float32)
    indices = jnp.arange(count // block, dtype=jnp.int32)
    (key_acc, value_acc), query_grads = lax.scan(one_block, (zeros, zeros), (indices, logsum))
    return (query_grads.reshape(query.shape), key_acc, value_acc)


def on_device(q_raw, k_raw, values, grad_out, q_gain, k_gain, lengths, positions):
    members = lax.axis_size("seq")
    replicas = lax.axis_size("dp")
    tok_dev = q_raw.shape[1]
    feature = q_raw.shape[2]
    tokens = tok_dev * members
    share = feature // members
    local_heads = share // HEAD_DIM
    reach = tokens // 3
    block = min(512, tokens)
    window = min(tokens, block + 2 * reach)
    segment = segment_ids(lengths[0], tokens)
    cosine, sine = rope_tables(positions[0], HEAD_DIM)
    query_float = q_raw[0].astype(jnp.float32)
    key_float = k_raw[0].astype(jnp.float32)
    query_scale = lax.rsqrt(jnp.mean(query_float * query_float, axis=-1) + epsilon)
    key_scale = lax.rsqrt(jnp.mean(key_float * key_float, axis=-1) + epsilon)
    query_hat = query_float * query_scale[:, None]
    key_hat = key_float * key_scale[:, None]
    query_rot = rotate_pairs((query_hat * q_gain).reshape(tok_dev, -1, HEAD_DIM), cosine, sine)
    key_rot = rotate_pairs((key_hat * k_gain).reshape(tok_dev, -1, HEAD_DIM), cosine, sine)
    sent = (
        query_rot.astype(jnp.bfloat16).reshape(1, tok_dev, feature),
        key_rot.astype(jnp.bfloat16).reshape(1, tok_dev, feature),
        values,
    )
    got_query, got_key, got_value = (
        lax.all_to_all(sent[0], "seq", split_axis=2, concat_axis=1, tiled=True),
        lax.all_to_all(sent[1], "seq", split_axis=2, concat_axis=1, tiled=True),
        lax.all_to_all(sent[2], "seq", split_axis=2, concat_axis=1, tiled=True),
    )
    query_heads = got_query[0].reshape(tokens, local_heads, HEAD_DIM)
    key_heads = got_key[0].reshape(tokens, local_heads, HEAD_DIM)
    value_heads = got_value[0].reshape(tokens, local_heads, HEAD_DIM)
    context, logsum = attention_forward(
        query_heads, key_heads, value_heads, segment, block, window, reach
    )
    context_half = context.astype(jnp.bfloat16)
    attended = lax.all_to_all(
        context_half.reshape(1, tokens, share), "seq", split_axis=1, concat_axis=2, tiled=True
    )
    cotangent = lax.all_to_all(grad_out, "seq", split_axis=2, concat_axis=1, tiled=True)[0].reshape(
        tokens, local_heads, HEAD_DIM
    )
    query_grad, key_grad, value_grad = attention_backward(
        query_heads,
        key_heads,
        value_heads,
        context_half,
        cotangent,
        logsum,
        segment,
        block,
        window,
        reach,
    )
    query_half = query_grad.astype(jnp.bfloat16)
    key_half = key_grad.astype(jnp.bfloat16)
    value_half = value_grad.astype(jnp.bfloat16).reshape(1, tokens, share)
    sent_back = (
        query_half.reshape(1, tokens, share),
        key_half.reshape(1, tokens, share),
        value_half,
    )
    back_query, back_key, back_value = (
        lax.all_to_all(sent_back[0], "seq", split_axis=1, concat_axis=2, tiled=True),
        lax.all_to_all(sent_back[1], "seq", split_axis=1, concat_axis=2, tiled=True),
        lax.all_to_all(sent_back[2], "seq", split_axis=1, concat_axis=2, tiled=True),
    )
    query_back = rotate_back(
        back_query[0].astype(jnp.float32).reshape(tok_dev, -1, HEAD_DIM), cosine, sine
    ).reshape(tok_dev, feature)
    key_back = rotate_back(
        back_key[0].astype(jnp.float32).reshape(tok_dev, -1, HEAD_DIM), cosine, sine
    ).reshape(tok_dev, feature)
    query_part = jnp.sum(query_back * query_hat, axis=0)
    key_part = jnp.sum(key_back * key_hat, axis=0)
    query_lift = query_back * q_gain
    key_lift = key_back * k_gain
    query_input = query_scale[:, None] * (
        query_lift - query_hat * jnp.mean(query_lift * query_hat, axis=-1, keepdims=True)
    )
    key_input = key_scale[:, None] * (
        key_lift - key_hat * jnp.mean(key_lift * key_hat, axis=-1, keepdims=True)
    )
    gains = lax.psum(jnp.stack([query_part, key_part]), ("dp", "seq")) / replicas
    grad_query_input = query_input.astype(jnp.bfloat16)[None]
    grad_key_input = key_input.astype(jnp.bfloat16)[None]
    return (attended, grad_query_input, grad_key_input, back_value, gains[0], gains[1])


def solution(mesh):
    return jax.shard_map(
        on_device,
        mesh=mesh,
        in_specs=(
            P("dp", "seq", None),
            P("dp", "seq", None),
            P("dp", "seq", None),
            P("dp", "seq", None),
            P(),
            P(),
            P("dp", None),
            P("dp", None, "seq"),
        ),
        out_specs=(
            P("dp", "seq", None),
            P("dp", "seq", None),
            P("dp", "seq", None),
            P("dp", "seq", None),
            P(),
            P(),
        ),
        check_vma=False,
    )
```

profile of v0, /device:TPU:0, one launch (start us, length us, event | category | flops | bytes accessed | tf_op | source)
XLA Modules:
  0.0 501.7 jit_solution(1113454433465873790)
XLA Ops:
  12.2 16.7 %copy.213 = bf16[1,128,4096]{1,0,2:T(2,128)(2,1)S(1)} copy(bf16[1,128,4096]{1,2,0:T(8,128)(2,1)S(1)} %get-tuple-element.342) | data formatting | bytes 2097152 | tf_op jit(solution)/shard_map/convert_element_type | solution.py:157
  29.4 23.4 %reduce.10 = bf16[4096,128]{1,0:T(8,128)(2,1)} reduce(bf16[4096,1,128]{2,1,0:T(2,128)(2,1)S(1)} %bitcast.238, bf16[]{:T(256)} %broadcast.330), dimensions={1}, to_apply=%bitcast.188.reduce_sub_computation | reduce | bytes 2097154
  54.9 7.5 %all-to-all-start = ((bf16[8,2,32768]{2,1,0:T(2,128)(2,1)}), bf16[8,2,32768]{2,1,0:T(2,128)(2,1)}, u32[]{:S(2)}, u32[]{:S(2)}) async-start(bf16[8,2,32768]{2,1,0:T(2,128)(2,1)} %reshape.589), calls=%async_computation | async-start | bytes 2097152 | tf_op jit(solution)/shard_map/all_to_all | solution.py:162
  62.5 16.7 %copy.212 = bf16[1,128,4096]{1,0,2:T(2,128)(2,1)S(1)} copy(bf16[1,128,4096]{1,2,0:T(8,128)(2,1)S(1)} %get-tuple-element.341) | data formatting | bytes 2097152 | tf_op jit(solution)/shard_map/convert_element_type | solution.py:158
  79.2 22.4 %reduce.11 = bf16[4096,128]{1,0:T(8,128)(2,1)S(1)} reduce(bf16[4096,1,128]{2,1,0:T(2,128)(2,1)S(1)} %bitcast.241, bf16[]{:T(256)} %broadcast.330), dimensions={1}, to_apply=%bitcast.187.reduce_sub_computation | reduce | bytes 2097154
  102.7 6.0 %all-to-all-start.1 = ((bf16[8,2,32768]{2,1,0:T(2,128)(2,1)}), bf16[8,2,32768]{2,1,0:T(2,128)(2,1)S(1)}, u32[]{:S(2)}, u32[]{:S(2)}) async-start(bf16[8,2,32768]{2,1,0:T(2,128)(2,1)} %reshape.591), calls=%async_computation.1 | async-start | bytes 2097152 | tf_op jit(solution)/shard_map/all_to_all | solution.py:163
  113.8 23.4 %reduce.12 = bf16[4096,128]{1,0:T(8,128)(2,1)} reduce(bf16[4096,1,128]{2,1,0:T(2,128)(2,1)S(1)} %bitcast.245, bf16[]{:T(256)} %broadcast.330), dimensions={1}, to_apply=%bitcast.164.reduce_sub_computation | reduce | bytes 2097154
  139.3 6.3 %all-to-all-start.2 = ((bf16[8,2,32768]{2,1,0:T(2,128)(2,1)}), bf16[8,2,32768]{2,1,0:T(2,128)(2,1)}, u32[]{:S(2)}, u32[]{:S(2)}) async-start(bf16[8,2,32768]{2,1,0:T(2,128)(2,1)} %reshape.593), calls=%async_computation.2 | async-start | bytes 2097152 | tf_op jit(solution)/shard_map/all_to_all | solution.py:164
  145.8 5.5 %copy.167 = bf16[1,128,4096]{1,0,2:T(2,128)(2,1)} copy(bf16[1,128,4096]{2,1,0:T(8,128)(2,1)} %param.15) | data formatting | bytes 2097152 | tf_op args[3]
  151.3 24.4 %reduce.14 = bf16[4096,128]{1,0:T(8,128)(2,1)} reduce(bf16[4096,1,128]{2,1,0:T(2,128)(2,1)} %bitcast.246, bf16[]{:T(256)} %broadcast.330), dimensions={1}, to_apply=%bitcast.168.reduce_sub_computation | reduce | bytes 2097154
  177.9 5.8 %reshape.590 = bf16[4096,1,128]{2,1,0:T(2,128)(2,1)} reshape(bf16[8,2,32768]{2,1,0:T(2,128)(2,1)} %all-to-all-done) | data formatting | bytes 2097152
  200.4 6.5 %all-to-all-start.4 = ((bf16[8,2,32768]{2,1,0:T(2,128)(2,1)}), bf16[8,2,32768]{2,1,0:T(2,128)(2,1)}, u32[]{:S(2)}, u32[]{:S(2)}) async-start(bf16[8,2,32768]{2,1,0:T(2,128)(2,1)} %reshape.597), calls=%async_computation.4 | async-start | bytes 2097152 | tf_op jit(solution)/shard_map/all_to_all | solution.py:176
  206.8 5.8 %reshape.594 = bf16[4096,1,128]{2,1,0:T(2,128)(2,1)} reshape(bf16[8,2,32768]{2,1,0:T(2,128)(2,1)} %all-to-all-done.2) | data formatting | bytes 2097152
  221.7 21.2 %while.27 = (s32[]{:T(128)}, bf16[2,512,4,128]{3,1,2,0:T(8,128)(2,1)}, f32[2,4,512]{2,1,0:T(4,128)S(1)}, s32[2]{0:T(128)S(1)}, s32[1024]{0:T(1024)S(1)}, /*index...) while((s32[]{:T(128)}, ...), condition=%wide.region_7.8_spmd, body=%wide.region_4.7_spmd.sunk | while | flops 1099429888 | bytes 35203796 | solution.py:81
  250.7 5.8 %reshape.598 = bf16[4096,1,128]{2,1,0:T(2,128)(2,1)} reshape(bf16[8,2,32768]{2,1,0:T(2,128)(2,1)} %all-to-all-done.4) | data formatting | bytes 2097152
  265.4 47.3 %while.28 = (s32[]{:T(128)}, f32[1024,4,128]{0,2,1:T(8,128)S(1)}, f32[1024,4,128]{0,2,1:T(8,128)}, bf16[2,512,4,128]{3,1,2,0:T(8,128)(2,1)}, s32[2]{0:T(128)S(1)...) while((s32[]{:T(128)}, f32[1024,4,128]{0,2,1:T(8,128)S(1)}, ...), condition=%wide.region_10.11_spmd.clone, body=%wide.region_9.10_spmd.clone.sunk | while | flops 2710044672 | bytes 154733552 | solution.py:131
  318.1 8.0 %reduce.16 = bf16[1024,512]{1,0:T(8,128)(2,1)S(1)} reduce(bf16[1024,1,512]{2,1,0:T(2,128)(2,1)} %bitcast.242, bf16[]{:T(256)} %broadcast.330), dimensions={1}, to_apply=%bitcast.170.reduce_sub_computation | reduce | bytes 2097154
  327.7 6.3 %all-to-all-start.5 = ((bf16[8,2,32768]{2,1,0:T(2,128)(2,1)}), bf16[8,2,32768]{2,1,0:T(2,128)(2,1)}, u32[]{:S(2)}, u32[]{:S(2)}) async-start(bf16[8,2,32768]{2,1,0:T(2,128)(2,1)} %reshape.599), calls=%async_computation.5 | async-start | bytes 2097152 | tf_op jit(solution)/shard_map/all_to_all | solution.py:200
  336.1 7.0 %reduce.15 = bf16[1024,512]{1,0:T(8,128)(2,1)S(1)} reduce(bf16[1024,1,512]{2,1,0:T(2,128)(2,1)S(1)} %bitcast.243, bf16[]{:T(256)} %broadcast.330), dimensions={1}, to_apply=%bitcast.172.reduce_sub_computation | reduce | bytes 2097154
  344.7 13.1 %all-to-all-done.5 = bf16[8,2,32768]{2,1,0:T(2,128)(2,1)} async-done(((bf16[8,2,32768]{2,1,0:T(2,128)(2,1)}), bf16[8,2,32768]{2,1,0:T(2,128)(2,1)}, u32[]{:S(2)}, u32[]{:S(2)}) %all-to-all-start.5) | async-done | bytes 1048608 | tf_op jit(solution)/shard_map/all_to_all | solution.py:200
  374.4 8.1 %reduce.17 = bf16[1024,512]{1,0:T(8,128)(2,1)} reduce(bf16[1024,1,512]{2,1,0:T(2,128)(2,1)S(1)} %bitcast.244, bf16[]{:T(256)} %broadcast.330), dimensions={1}, to_apply=%bitcast.174.reduce_sub_computation | reduce | bytes 2097154
  385.7 7.0 %reduce.13 = bf16[1024,512]{1,0:T(8,128)(2,1)S(1)} reduce(bf16[1024,1,512]{2,1,0:T(2,128)(2,1)S(1)} %bitcast.240, bf16[]{:T(256)} %broadcast.330), dimensions={1}, to_apply=%bitcast.166.reduce_sub_computation | reduce | bytes 2097154
  403.6 6.0 %all-to-all-start.7 = ((bf16[8,2,32768]{2,1,0:T(2,128)(2,1)}), bf16[8,2,32768]{2,1,0:T(2,128)(2,1)}, u32[]{:S(2)}, u32[]{:S(2)}) async-start(bf16[8,2,32768]{2,1,0:T(2,128)(2,1)} %reshape.603), calls=%async_computation.7 | async-start | bytes 2097152 | tf_op jit(solution)/shard_map/all_to_all | solution.py:202
  453.4 40.8 %psum.7 = f32[2,4096]{1,0:T(2,128)S(1)} all-reduce(f32[2,4096]{1,0:T(2,128)S(1)} %pad_maximum_fusion.4), channel_id=1, replica_groups=mesh['dp'=4,'seq'=8] {'dp','seq'}, use_global_device_ids=true, to_apply=%region_15.16 | all-reduce | flops 8192 | bytes 65536 | tf_op jit(solution)/shard_map/psum | solution.py:220
  (236 shorter events, 224.5 us)
Async XLA Ops:
  2.3 8.3 %copy-start.3 = (bf16[1,128,4096]{1,2,0:T(8,128)(2,1)}, bf16[1,128,4096]{1,2,0:T(8,128)(2,1)S(1)}, u32[]{:S(2)}) copy-start(bf16[1,128,4096]{1,2,0:T(8,128)(2,1)S(1)} %copy.156) | copy-start | bytes 3145732
  5.0 5.6 %copy-start.5 = (bf16[1,128,4096]{1,2,0:T(8,128)(2,1)}, bf16[1,128,4096]{1,2,0:T(8,128)(2,1)S(1)}, u32[]{:S(2)}) copy-start(bf16[1,128,4096]{1,2,0:T(8,128)(2,1)S(1)} %copy.153) | copy-start | bytes 3145732
  5.8 4.8 copy-start.31
  5.8 4.8 copy-start.33
  54.9 47.8 %all-to-all-start = ((bf16[8,2,32768]{2,1,0:T(2,128)(2,1)}), bf16[8,2,32768]{2,1,0:T(2,128)(2,1)}, u32[]{:S(2)}, u32[]{:S(2)}) async-start(bf16[8,2,32768]{2,1,0:T(2,128)(2,1)} %reshape.589), calls=%async_computation | async-start | bytes 2097152 | tf_op jit(solution)/shard_map/all_to_all | solution.py:162
  102.7 36.5 %all-to-all-start.1 = ((bf16[8,2,32768]{2,1,0:T(2,128)(2,1)}), bf16[8,2,32768]{2,1,0:T(2,128)(2,1)S(1)}, u32[]{:S(2)}, u32[]{:S(2)}) async-start(bf16[8,2,32768]{2,1,0:T(2,128)(2,1)} %reshape.591), calls=%async_computation.1 | async-start | bytes 2097152 | tf_op jit(solution)/shard_map/all_to_all | solution.py:163
  137.1 8.4 %copy-start.36 = (s32[1,6]{1,0:T(1,128)S(1)}, s32[1,6]{1,0:T(1,128)}, u32[]{:S(2)}) copy-start(s32[1,6]{1,0:T(1,128)} %param.18) | copy-start | bytes 76
  139.3 61.1 %all-to-all-start.2 = ((bf16[8,2,32768]{2,1,0:T(2,128)(2,1)}), bf16[8,2,32768]{2,1,0:T(2,128)(2,1)}, u32[]{:S(2)}, u32[]{:S(2)}) async-start(bf16[8,2,32768]{2,1,0:T(2,128)(2,1)} %reshape.593), calls=%async_computation.2 | async-start | bytes 2097152 | tf_op jit(solution)/shard_map/all_to_all | solution.py:164
  200.4 50.3 %all-to-all-start.4 = ((bf16[8,2,32768]{2,1,0:T(2,128)(2,1)}), bf16[8,2,32768]{2,1,0:T(2,128)(2,1)}, u32[]{:S(2)}, u32[]{:S(2)}) async-start(bf16[8,2,32768]{2,1,0:T(2,128)(2,1)} %reshape.597), calls=%async_computation.4 | async-start | bytes 2097152 | tf_op jit(solution)/shard_map/all_to_all | solution.py:176
  266.8 5.9 %copy-start.15 = (bf16[1024,4,128]{0,2,1:T(8,128)(2,1)S(1)}, bf16[1024,4,128]{0,2,1:T(8,128)(2,1)}, u32[]{:S(2)}) copy-start(bf16[1024,4,128]{0,2,1:T(8,128)(2,1)} %get-tuple-element.556) | copy-start | bytes 3145732 | tf_op jit(solution)/shard_map/while
  266.9 5.9 %copy-start.24 = (bf16[1024,4,128]{2,0,1:T(8,128)(2,1)S(1)}, bf16[1024,4,128]{2,0,1:T(8,128)(2,1)}, u32[]{:S(2)}) copy-start(bf16[1024,4,128]{2,0,1:T(8,128)(2,1)} %get-tuple-element.557) | copy-start | bytes 3145732 | tf_op jit(solution)/shard_map/while
  277.8 6.2 %copy-start.2 = (f32[4,512,1024]{2,1,0:T(8,128)S(1)}, f32[4,512,1024]{2,1,0:T(8,128)}, u32[]{:S(2)}) copy-start(f32[4,512,1024]{2,1,0:T(8,128)} %copy-done.1) | copy-start | bytes 25165828 | tf_op jit(solution)/shard_map/while
  289.8 5.9 %copy-start.15 = (bf16[1024,4,128]{0,2,1:T(8,128)(2,1)S(1)}, bf16[1024,4,128]{0,2,1:T(8,128)(2,1)}, u32[]{:S(2)}) copy-start(bf16[1024,4,128]{0,2,1:T(8,128)(2,1)} %get-tuple-element.556) | copy-start | bytes 3145732 | tf_op jit(solution)/shard_map/while
  289.8 5.9 %copy-start.24 = (bf16[1024,4,128]{2,0,1:T(8,128)(2,1)S(1)}, bf16[1024,4,128]{2,0,1:T(8,128)(2,1)}, u32[]{:S(2)}) copy-start(bf16[1024,4,128]{2,0,1:T(8,128)(2,1)} %get-tuple-element.557) | copy-start | bytes 3145732 | tf_op jit(solution)/shard_map/while
  300.8 6.2 %copy-start.2 = (f32[4,512,1024]{2,1,0:T(8,128)S(1)}, f32[4,512,1024]{2,1,0:T(8,128)}, u32[]{:S(2)}) copy-start(f32[4,512,1024]{2,1,0:T(8,128)} %copy-done.1) | copy-start | bytes 25165828 | tf_op jit(solution)/shard_map/while
  327.7 30.1 %all-to-all-start.5 = ((bf16[8,2,32768]{2,1,0:T(2,128)(2,1)}), bf16[8,2,32768]{2,1,0:T(2,128)(2,1)}, u32[]{:S(2)}, u32[]{:S(2)}) async-start(bf16[8,2,32768]{2,1,0:T(2,128)(2,1)} %reshape.599), calls=%async_computation.5 | async-start | bytes 2097152 | tf_op jit(solution)/shard_map/all_to_all | solution.py:200
  343.1 19.4 %copy-start.30 = (f32[4096]{0:T(1024)S(1)}, f32[4096]{0:T(1024)}, u32[]{:S(2)}) copy-start(f32[4096]{0:T(1024)} %param.16) | copy-start | bytes 49156
  343.1 19.5 %copy-start.28 = (f32[4096]{0:T(1024)S(1)}, f32[4096]{0:T(1024)}, u32[]{:S(2)}) copy-start(f32[4096]{0:T(1024)} %param.17) | copy-start | bytes 49156
  343.1 19.5 %copy-start.21 = (f32[128,128]{0,1:T(8,128)S(1)}, f32[128,128]{0,1:T(8,128)}, u32[]{:S(2)}) copy-start(f32[128,128]{0,1:T(8,128)} %copy-done.20) | copy-start | bytes 196612
  357.8 45.8 %all-to-all-start.6 = ((bf16[8,2,32768]{2,1,0:T(2,128)(2,1)}), bf16[8,2,32768]{2,1,0:T(2,128)(2,1)}, u32[]{:S(2)}, u32[]{:S(2)}) async-start(bf16[8,2,32768]{2,1,0:T(2,128)(2,1)} %reshape.601), calls=%async_computation.6 | async-start | bytes 2097152 | tf_op jit(solution)/shard_map/all_to_all | solution.py:201
  374.3 10.7 %copy-start.17 = (bf16[2,512,4,128]{3,2,1,0:T(4,128)(2,1)S(1)}, bf16[2,512,4,128]{3,2,1,0:T(4,128)(2,1)}, u32[]{:S(2)}) copy-start(bf16[2,512,4,128]{3,2,1,0:T(4,128)(2,1)} %copy.164) | copy-start | bytes 3145732
  403.6 30.2 %all-to-all-start.7 = ((bf16[8,2,32768]{2,1,0:T(2,128)(2,1)}), bf16[8,2,32768]{2,1,0:T(2,128)(2,1)}, u32[]{:S(2)}, u32[]{:S(2)}) async-start(bf16[8,2,32768]{2,1,0:T(2,128)(2,1)} %reshape.603), calls=%async_computation.7 | async-start | bytes 2097152 | tf_op jit(solution)/shard_map/all_to_all | solution.py:202
  431.4 6.9 %copy-start.4 = (bf16[1,128,4096]{1,2,0:T(8,128)(2,1)S(1)}, bf16[1,128,4096]{1,2,0:T(8,128)(2,1)}, u32[]{:S(2)}) copy-start(bf16[1,128,4096]{1,2,0:T(8,128)(2,1)} %copy-done.3) | copy-start | bytes 3145732
  433.9 61.0 %all-to-all-start.3 = ((bf16[8,2,32768]{2,1,0:T(2,128)(2,1)}), bf16[8,2,32768]{2,1,0:T(2,128)(2,1)}, u32[]{:S(2)}, u32[]{:S(2)}) async-start(bf16[8,2,32768]{2,1,0:T(2,128)(2,1)} %reshape.595), calls=%async_computation.3 | async-start | bytes 2097152 | tf_op jit(solution)/shard_map/all_to_all | solution.py:173
  (30 other events, 76.9 us)
where the time goes:
time: 511 us; the launch traced here: 502 us
  local copies, waits for them, and re-layouts  186 us (36%)
  other arithmetic  159 us (31%)
  matrix products  48.8 us (10%)
  starting transfers between devices  47.7 us (9%)
  blocking collectives  40.8 us (8%)
  waiting for transfers between devices  15.5 us (3%)
    unnamed x10, other arithmetic  124 us
    unnamed x89, local copies, waits for them, and re-layouts  85 us
    dot_general x14, matrix products, product(): return jnp.einsum(form, left, right, preferred_element_type=jnp.float32)  48.5 us
    psum x1, blocking collectives, on_device(): lax.psum(jnp.stack([query_part, key_part]), ('dp', 'seq')) / replicas  40.8 us
    convert_element_type x1, local copies, waits for them, and re-layouts, on_device(): query_rot.astype(jnp.bfloat16).reshape(1, tok_dev, feature)  16.7 us
    convert_element_type x1, local copies, waits for them, and re-layouts, on_device(): key_rot.astype(jnp.bfloat16).reshape(1, tok_dev, feature)  16.7 us
    all_to_all x1, waiting for transfers between devices, on_device(): lax.all_to_all(sent_back[0], 'seq', split_axis=1, concat_axis=2, tiled=True)  13.1 us
  transfers between devices with their start and end apart: 8, of which 2 were waited for; matrix products, arithmetic and copies ran while one was open for 51% of the time, Pallas kernels for 0%

commit v1 on v0

v1 whole, which is shorter than its diff:
```python
import functools

import jax
import jax.numpy as jnp
import numpy as np
from jax import lax
from jax.experimental import pallas as pl
from jax.experimental.pallas import tpu as pltpu
from jax.sharding import PartitionSpec as P

HEAD_DIM = 128
LANES = 128
QUERY_BLOCK = 256
EPSILON = 1e-06
MESH = pl.DeviceIdType.MESH


def rope_tables(position_rows, head_dim):
    half = head_dim // 2
    sixth = head_dim // 6
    first = half - 2 * sixth
    pairs = np.arange(head_dim) % half
    section = (pairs >= first).astype(np.int32) + (pairs >= first + sixth).astype(np.int32)
    begin = np.where(section == 0, 0, np.where(section == 1, first, first + sixth))
    number = np.where(section == 0, first, sixth)
    freqs = (10000.0 ** (-(pairs - begin) / number)).astype(np.float32)
    sign = np.where(np.arange(head_dim) < half, -1.0, 1.0).astype(np.float32)
    rows = position_rows.astype(jnp.float32)[:, :, None]
    chosen = jnp.where(section == 0, rows[0], jnp.where(section == 1, rows[1], rows[2]))
    angle = chosen * freqs
    return jnp.cos(angle), jnp.sin(angle) * sign


def dot(left, right, left_dim, right_dim):
    return lax.dot_general(
        left, right, (((left_dim,), (right_dim,)), ((), ())), preferred_element_type=jnp.float32
    )


def kernel(
    sizes,
    len_ref, q_ref, k_ref, v_ref, do_ref, gq_ref, gk_ref, cos_ref, sin_ref,
    out_ref, gain_ref,
    sent, recv, back, key_acc, value_acc, scale_q, scale_k,
    part, seq_part, dp_sum, dp_part, total,
    in_send, in_recv, own_sem, out_send, out_recv, gain_send, gain_recv,
):
    n, replicas, heads, tok, clips, reach = sizes
    tokens = n * tok
    feature = n * heads * HEAD_DIM
    me = lax.axis_index("seq")
    my_dp = lax.axis_index("dp")
    scale = HEAD_DIM ** (-0.5)

    def peer(step):
        return lax.rem(me + step, n)

    def columns(owner, head):
        return pl.ds(pl.multiple_of((owner * heads + head) * HEAD_DIM, HEAD_DIM), HEAD_DIM)

    def rows(owner):
        return pl.ds(pl.multiple_of(owner * tok, tok), tok)

    def remote(src, dst, send_sem, recv_sem, device):
        return pltpu.make_async_remote_copy(
            src_ref=src, dst_ref=dst, send_sem=send_sem, recv_sem=recv_sem,
            device_id=device, device_id_type=MESH,
        )

    barrier = pltpu.get_barrier_semaphore()
    for step in range(1, n):
        pl.semaphore_signal(barrier, inc=1, device_id=(my_dp, peer(step)), device_id_type=MESH)
    for step in range(1, replicas):
        other = lax.rem(my_dp + step, replicas)
        pl.semaphore_signal(barrier, inc=1, device_id=(other, me), device_id_type=MESH)
    pl.semaphore_wait(barrier, n - 1 + replicas - 1)

    def send_values(head):
        pltpu.make_async_copy(
            v_ref.at[:, columns(me, head)], recv.at[head, 2, rows(me), :], own_sem.at[head]
        ).start()
        pltpu.make_async_copy(
            do_ref.at[:, columns(me, head)], recv.at[head, 3, rows(me), :], own_sem.at[head]
        ).start()

        @pl.loop(1, n)
        def _(step):
            other = peer(step)
            for place, ref in ((2, v_ref), (3, do_ref)):
                remote(
                    ref.at[:, columns(other, head)], recv.at[head, place, rows(me), :],
                    in_send.at[head], in_recv.at[head], (my_dp, other),
                ).start()

    send_values(0)

    def squares(index, sums):
        cols = pl.ds(pl.multiple_of(index * LANES, LANES), LANES)
        query = q_ref[:, cols].astype(jnp.float32)
        keys = k_ref[:, cols].astype(jnp.float32)
        return sums[0] + query * query, sums[1] + keys * keys

    zero = jnp.zeros((tok, LANES), jnp.float32)
    sum_q, sum_k = lax.fori_loop(0, feature // LANES, squares, (zero, zero))
    for sums, target in ((sum_q, scale_q), (sum_k, scale_k)):
        mean = jnp.sum(sums, axis=1, keepdims=True) / feature
        target[...] = jnp.broadcast_to(lax.rsqrt(mean + EPSILON), (tok, LANES))

    def rotated(ref, gain, norm, cols):
        x = ref[:, cols].astype(jnp.float32) * norm[...] * gain[:, cols]
        turned = x * cos_ref[...] + pltpu.roll(x, HEAD_DIM // 2, 1) * sin_ref[...]
        return turned.astype(jnp.bfloat16)

    for head in range(heads):
        if head:
            send_values(head)

        @pl.loop(1, n)
        def _(step):
            other = peer(step)
            cols = columns(other, head)
            sent[head, other, 0] = rotated(q_ref, gq_ref, scale_q, cols)
            sent[head, other, 1] = rotated(k_ref, gk_ref, scale_k, cols)
            remote(
                sent.at[head, other], recv.at[head, 0:2, rows(me), :],
                in_send.at[head], in_recv.at[head], (my_dp, other),
            ).start()

        cols = columns(me, head)
        recv[head, 0, rows(me), :] = rotated(q_ref, gq_ref, scale_q, cols)
        recv[head, 1, rows(me), :] = rotated(k_ref, gk_ref, scale_k, cols)

    bounds = []
    running = len_ref[0, 0]
    for clip in range(clips):
        bounds.append(running)
        if clip + 1 < clips:
            running = running + len_ref[0, clip + 1]

    def segment(shape, dim, start):
        places = lax.broadcasted_iota(jnp.int32, shape, dim) + start
        found = jnp.zeros(shape, jnp.int32)
        for bound in bounds:
            found = found + (places >= bound).astype(jnp.int32)
        return found

    block = min(QUERY_BLOCK, tokens)

    @pl.loop(0, heads)
    def _(head):
        arrived = recv.at[head, :, pl.ds(0, (n - 1) * tok), :]
        pltpu.make_async_copy(arrived, arrived, in_recv.at[head]).wait()
        own = recv.at[head, pl.ds(2, 2), pl.ds(0, tok), :]
        pltpu.make_async_copy(own, own, own_sem.at[head]).wait()
        key_acc[...] = jnp.zeros_like(key_acc)
        value_acc[...] = jnp.zeros_like(value_acc)
        for start in range(0, tokens, block):
            low = max(0, start - reach) // LANES * LANES
            high = min(tokens, -(-(start + block + reach) // LANES) * LANES)
            query = recv[head, 0, start:start + block, :]
            keys = recv[head, 1, low:high, :]
            value_rows = recv[head, 2, low:high, :]
            cot = recv[head, 3, start:start + block, :]
            live = segment((block, 1), 0, start) == segment((1, high - low), 1, low)
            scores = jnp.where(live, dot(query, keys, 1, 1), -1e30)
            highest = jnp.max(scores, axis=1, keepdims=True)
            expon = jnp.exp((scores - highest) * scale)
            probs = expon * (1.0 / jnp.sum(expon, axis=1, keepdims=True))
            half = probs.astype(jnp.bfloat16)
            context = dot(half, value_rows, 1, 0).astype(jnp.bfloat16)
            delta = jnp.sum(
                cot.astype(jnp.float32) * context.astype(jnp.float32), axis=1, keepdims=True
            )
            dprob = dot(cot, value_rows, 1, 1)
            dscore = (probs * (dprob - delta) * scale).astype(jnp.bfloat16)
            back[head, 0, start:start + block, :] = context
            back[head, 1, start:start + block, :] = dot(dscore, keys, 1, 0).astype(jnp.bfloat16)
            key_acc[low:high, :] += dot(dscore, query, 0, 0)
            value_acc[low:high, :] += dot(half, cot, 0, 0)
        back[head, 2] = key_acc[...].astype(jnp.bfloat16)
        back[head, 3] = value_acc[...].astype(jnp.bfloat16)

        @pl.loop(1, n)
        def _(step):
            other = peer(step)
            remote(
                back.at[head, :, rows(other), :], out_ref.at[:, :, columns(me, head)],
                out_send.at[head], out_recv.at[head], (my_dp, other),
            ).start()

        out_ref[:, :, columns(me, head)] = back[head, :, rows(me), :]

    def turned_back(place, ref, norm, cols):
        grads = out_ref[place, :, cols].astype(jnp.float32)
        turned = grads * cos_ref[...] - pltpu.roll(grads, HEAD_DIM // 2, 1) * sin_ref[...]
        return turned, ref[:, cols].astype(jnp.float32) * norm[...]

    inner = (zero, zero)
    for head in range(heads):
        arrived = out_ref.at[:, :, pl.ds(0, (n - 1) * HEAD_DIM)]
        pltpu.make_async_copy(arrived, arrived, out_recv.at[head]).wait()

        def first_pass(owner, sums):
            cols = columns(owner, head)
            results = []
            for place, (ref, gain, norm) in enumerate(
                ((q_ref, gq_ref, scale_q), (k_ref, gk_ref, scale_k))
            ):
                turned, hat = turned_back(place + 1, ref, norm, cols)
                both = turned * hat
                row = place * heads + head
                part[owner, row:row + 1, :] = jnp.sum(both, axis=0, keepdims=True)
                results.append(sums[place] + both * gain[:, cols])
            return tuple(results)

        inner = lax.fori_loop(0, n, first_pass, inner)

    @pl.loop(1, n)
    def _(step):
        other = peer(step)
        remote(
            part.at[other], seq_part.at[me], gain_send.at[0], gain_recv.at[0], (my_dp, other)
        ).start()

    seq_part[me] = part[me]
    inner_q, inner_k = (
        jnp.broadcast_to(jnp.sum(sums, axis=1, keepdims=True) / feature, (tok, LANES))
        for sums in inner
    )

    def second_pass(index):
        cols = pl.ds(pl.multiple_of(index * LANES, LANES), LANES)
        for place, (ref, gain, norm, mean) in enumerate(
            ((q_ref, gq_ref, scale_q, inner_q), (k_ref, gk_ref, scale_k, inner_k))
        ):
            turned, hat = turned_back(place + 1, ref, norm, cols)
            result = norm[...] * (turned * gain[:, cols] - hat * mean)
            out_ref[place + 1, :, cols] = result.astype(jnp.bfloat16)

    pl.loop(0, feature // LANES)(second_pass)

    def wait_all(ref, count, sem):
        held = ref.at[pl.ds(0, count)]
        pltpu.make_async_copy(held, held, sem).wait()

    wait_all(seq_part, n - 1, gain_recv.at[0])
    dp_sum[...] = jnp.sum(seq_part[...], axis=0)
    for step in range(1, replicas):
        other = lax.rem(my_dp + step, replicas)
        remote(
            dp_sum, dp_part.at[my_dp], gain_send.at[1], gain_recv.at[1], (other, me)
        ).start()
    dp_part[my_dp] = dp_sum[...]
    wait_all(dp_part, replicas - 1, gain_recv.at[1])
    total[...] = jnp.sum(dp_part[...], axis=0) / replicas

    @pl.loop(1, n)
    def _(step):
        other = peer(step)
        remote(
            total, gain_ref.at[me], gain_send.at[2], gain_recv.at[2], (my_dp, other)
        ).start()

    gain_ref[me] = total[...]
    wait_all(gain_ref, n - 1, gain_recv.at[2])

    wait_all(seq_part, n - 1, gain_send.at[0])
    wait_all(dp_part, replicas - 1, gain_send.at[1])
    wait_all(seq_part, n - 1, gain_send.at[2])
    for head in range(heads):
        moved = recv.at[head, :, pl.ds(0, (n - 1) * tok), :]
        pltpu.make_async_copy(moved, moved, in_send.at[head]).wait()
        pltpu.make_async_copy(moved, moved, out_send.at[head]).wait()


def on_device(q_raw, k_raw, values, grad_out, q_gain, k_gain, lengths, positions):
    n = lax.axis_size("seq")
    replicas = lax.axis_size("dp")
    tok, feature = q_raw.shape[1:]
    heads = feature // n // HEAD_DIM
    tokens = n * tok
    reach = tokens // 3 - 1
    cosine, sine = rope_tables(positions[0], HEAD_DIM)
    sizes = (n, replicas, heads, tok, lengths.shape[1], reach)
    vmem = pl.BlockSpec(memory_space=pltpu.VMEM)
    hbm = pl.BlockSpec(memory_space=pl.ANY)
    gain_rows = (2 * heads, LANES)
    half, full = jnp.bfloat16, jnp.float32
    outs, gains = pl.pallas_call(
        functools.partial(kernel, sizes),
        out_shape=(
            jax.ShapeDtypeStruct((4, tok, feature), half),
            jax.ShapeDtypeStruct((n,) + gain_rows, full),
        ),
        in_specs=[
            pl.BlockSpec(memory_space=pltpu.SMEM), vmem, vmem, hbm, hbm, vmem, vmem, vmem, vmem,
        ],
        out_specs=(vmem, vmem),
        scratch_shapes=[
            pltpu.VMEM((heads, n, 2, tok, HEAD_DIM), half),
            pltpu.VMEM((heads, 4, tokens, HEAD_DIM), half),
            pltpu.VMEM((heads, 4, tokens, HEAD_DIM), half),
            pltpu.VMEM((tokens, HEAD_DIM), full),
            pltpu.VMEM((tokens, HEAD_DIM), full),
            pltpu.VMEM((tok, LANES), full),
            pltpu.VMEM((tok, LANES), full),
            pltpu.VMEM((n,) + gain_rows, full),
            pltpu.VMEM((n,) + gain_rows, full),
            pltpu.VMEM(gain_rows, full),
            pltpu.VMEM((replicas,) + gain_rows, full),
            pltpu.VMEM(gain_rows, full),
            pltpu.SemaphoreType.DMA((heads,)),
            pltpu.SemaphoreType.DMA((heads,)),
            pltpu.SemaphoreType.DMA((heads,)),
            pltpu.SemaphoreType.DMA((heads,)),
            pltpu.SemaphoreType.DMA((heads,)),
            pltpu.SemaphoreType.DMA((3,)),
            pltpu.SemaphoreType.DMA((3,)),
        ],
        compiler_params=pltpu.CompilerParams(
            collective_id=0, has_side_effects=True, vmem_limit_bytes=56 * 1024 * 1024
        ),
    )(
        lengths, q_raw[0], k_raw[0], values[0], grad_out[0],
        q_gain[None], k_gain[None], cosine, sine,
    )
    gains = gains.reshape(n, 2, heads * HEAD_DIM)
    return (
        outs[0][None], outs[1][None], outs[2][None], outs[3][None],
        gains[:, 0].reshape(feature), gains[:, 1].reshape(feature),
    )


def solution(mesh):
    tokens = P("dp", "seq", None)
    return jax.shard_map(
        on_device,
        mesh=mesh,
        in_specs=(tokens, tokens, tokens, tokens, P(), P(), P("dp", None), P("dp", None, "seq")),
        out_specs=(tokens, tokens, tokens, tokens, P(), P()),
        check_vma=False,
    )
```

time: 511 us -> 212 us (0.41); the launches traced: 502 us -> 212 us
  Pallas kernels: 0 us -> 204 us
  local copies, waits for them, and re-layouts: 186 us -> 4.95 us
  other arithmetic: 159 us -> 2.39 us
  matrix products: 48.8 us -> 0 us
  starting transfers between devices: 47.7 us -> 0 us
  blocking collectives: 40.8 us -> 0 us
  waiting for transfers between devices: 15.5 us -> 0 us
    pallas_call x0 -> x1, Pallas kernels: none -> 204 us  [on_device(): pl.pallas_call(functools.partial(kernel, sizes), out_shape=(jax.ShapeDtyp...]
    unnamed x10 -> x0, other arithmetic: 124 us -> none
    unnamed x89 -> x2, local copies, waits for them, and re-layouts: 85 us -> 0.01 us
    convert_element_type x11 -> x0, local copies, waits for them, and re-layouts: 56.7 us -> none  [the longest x1 16.7 us: on_device(): query_rot.astype(jnp.bfloat16).reshape(1, tok_dev, feature)]
    dot_general x15 -> x0, matrix products: 48.8 us -> none  [the longest x14 48.5 us: product(): return jnp.einsum(form, left, right, preferred_element_type=jnp.float32)]
    all_to_all x8 -> x0, starting transfers between devices: 47.7 us -> none  [the longest x1 7.54 us: on_device(): lax.all_to_all(sent[0], 'seq', split_axis=2, concat_axis=1, tiled=True)]
    psum x1 -> x0, blocking collectives: 40.8 us -> none  [on_device(): lax.psum(jnp.stack([query_part, key_part]), ('dp', 'seq')) / replicas]
    all_to_all x8 -> x0, waiting for transfers between devices: 15.5 us -> none  [the longest x1 13.1 us: on_device(): lax.all_to_all(sent_back[0], 'seq', split_axis=1, concat_axis=2, tiled=True)]
  transfers between devices with their start and end apart: 8 -> 0, of which waited for: 2 -> 0; matrix products, arithmetic and copies ran while one was open for 51% -> 0% of each run, Pallas kernels for 0% -> 0%
where the time goes in v1:
time: 212 us
  Pallas kernels  204 us (96%)
  local copies, waits for them, and re-layouts  4.95 us (2%)
  other arithmetic  2.39 us (1%)
    pallas_call x1, Pallas kernels, on_device(): pl.pallas_call(functools.partial(kernel, sizes), out_shape=(jax.ShapeDtyp...  204 us
    slice x1, local copies, waits for them, and re-layouts, on_device(): outs[3][None]  4.28 us

profile of v1, /device:TPU:0, one launch (start us, length us, event | category | flops | bytes accessed | tf_op | source)
XLA Modules:
  0.0 211.9 jit_solution(5926894316428048864)
XLA Ops:
  0.6 0.7 convert_element_type.4
  1.3 1.7 sine_multiply_fusion
  3.0 203.9 %shard_map.163 = (bf16[4,128,4096]{2,1,0:T(8,128)(2,1)}, f32[8,8,128]{2,1,0:T(8,128)}) custom-call(s32[1,6]{1,0:T(1,128)} %len_ref.1, bf16[128,4096]{1,0:T(8,128)(2,1)} %bitcast.14, bf16[128,4096]{1,0:T(8,128)(2,1)} %bitcast.15, bf16[128,4096]{1,0:T(8,128)(2,1)} %bitcast.16, bf16[128,4096]{1,0:T(8,128)(2,1)} %bitcast.17, f32[1,4096]{1,0:T(1,128)} %bitcast.18, ...), custom_call_target="tpu_custom_call" | custom-call | tf_op jit(solution)/shard_map/pallas_call | solution.py:289
  206.9 0.0 copy-start
  207.0 4.3 %fusion.1 = (bf16[1,128,4096]{2,1,0:T(8,128)(2,1)}, bf16[1,128,4096]{2,1,0:T(8,128)(2,1)}, bf16[1,128,4096]{2,1,0:T(8,128)(2,1)}, bf16[1,128,4096]{2,1,0:T(8,128)(2,1)}) fusion(bf16[4,128,4096]{2,1,0:T(8,128)(2,1)} %get-tuple-element.8), kind=kLoop, calls=%fused_computation.6 | loop fusion | bytes 8388608 | tf_op jit(solution)/shard_map/slice | solution.py:329
  211.2 0.0 copy-done
  211.3 0.6 fusion.2
  (2 shorter events, 0.0 us)
Async XLA Ops:
  206.9 4.3 %copy-start = (f32[8,8,128]{2,1,0:T(8,128)S(1)}, f32[8,8,128]{2,1,0:T(8,128)}, u32[]{:S(2)}) copy-start(f32[8,8,128]{2,1,0:T(8,128)} %get-tuple-element.9) | copy-start | bytes 98308

commit v2 on v1

--- a/solution.py
+++ b/solution.py
@@ -41,25 +41,49 @@
     sizes,
     len_ref, q_ref, k_ref, v_ref, do_ref, gq_ref, gk_ref, cos_ref, sin_ref,
     out_ref, gain_ref,
-    sent, recv, back, key_acc, value_acc, scale_q, scale_k,
+    other_out, sent, recv, back, key_acc, value_acc, scale_q, scale_k,
     part, seq_part, dp_sum, dp_part, total,
     in_send, in_recv, own_sem, out_send, out_recv, gain_send, gain_recv,
+    cross_in_send, cross_out_send, cross_out_recv,
 ):
-    n, replicas, heads, tok, clips, reach = sizes
-    tokens = n * tok
-    feature = n * heads * HEAD_DIM
+    n, replicas, heads, tok, clips, reach, halo, padded = sizes
+    members = n // 2
+    half_tokens = members * tok
+    window = half_tokens + halo
+    feature = members * heads * HEAD_DIM
+    shared = heads // 2
     me = lax.axis_index("seq")
+    side = me // members
+    place_in = lax.rem(me, members)
+    base = side * halo
+    crossing = [(d, min(tok, halo - d * tok)) for d in range(-(-halo // tok))]
     my_dp = lax.axis_index("dp")
     scale = HEAD_DIM ** (-0.5)
 
     def peer(step):
         return lax.rem(me + step, n)
 
+    def member(step):
+        return lax.rem(place_in + step, members)
+
+    def device(group, index):
+        return (my_dp, group * members + index)
+
     def columns(owner, head):
         return pl.ds(pl.multiple_of((owner * heads + head) * HEAD_DIM, HEAD_DIM), HEAD_DIM)
 
     def rows(owner):
-        return pl.ds(pl.multiple_of(owner * tok, tok), tok)
+        return pl.ds(pl.multiple_of(base + owner * tok, 16), tok)
+
+    def each_crossing(act):
+        for d, count in crossing:
+            @pl.when(me == members - 1 - d)
+            def _():
+                act(1, slice(tok - count, tok), slice(halo - d * tok - count, halo - d * tok), count)
+
+            @pl.when(me == members + d)
+            def _():
+                act(0, slice(0, count), slice(half_tokens + d * tok, half_tokens + d * tok + count), count)
 
     def remote(src, dst, send_sem, recv_sem, device):
         return pltpu.make_async_remote_copy(
@@ -76,20 +100,31 @@
     pl.semaphore_wait(barrier, n - 1 + replicas - 1)
 
     def send_values(head):
-        pltpu.make_async_copy(
-            v_ref.at[:, columns(me, head)], recv.at[head, 2, rows(me), :], own_sem.at[head]
-        ).start()
-        pltpu.make_async_copy(
-            do_ref.at[:, columns(me, head)], recv.at[head, 3, rows(me), :], own_sem.at[head]
-        ).start()
-
-        @pl.loop(1, n)
+        cols = columns(place_in, head)
+        for place, ref in ((2, v_ref), (3, do_ref)):
+            pltpu.make_async_copy(
+                ref.at[:, cols], recv.at[head, place, rows(place_in), :], own_sem.at[head]
+            ).start()
+
+        def cross(group, source, target, count):
+            @pl.loop(0, members)
+            def _(step):
+                other = member(step)
+                for place, ref in ((2, v_ref), (3, do_ref)):
+                    remote(
+                        ref.at[source, columns(other, head)], recv.at[head, place, target, :],
+                        cross_in_send.at[head], in_recv.at[head], device(group, other),
+                    ).start()
+
+        each_crossing(cross)
+
+        @pl.loop(1, members)
         def _(step):
-            other = peer(step)
+            other = member(step)
             for place, ref in ((2, v_ref), (3, do_ref)):
                 remote(
-                    ref.at[:, columns(other, head)], recv.at[head, place, rows(me), :],
-                    in_send.at[head], in_recv.at[head], (my_dp, other),
+                    ref.at[:, columns(other, head)], recv.at[head, place, rows(place_in), :],
+                    in_send.at[head], in_recv.at[head], device(side, other),
                 ).start()
 
     send_values(0)
@@ -111,24 +146,39 @@
         turned = x * cos_ref[...] + pltpu.roll(x, HEAD_DIM // 2, 1) * sin_ref[...]
         return turned.astype(jnp.bfloat16)
 
-    for head in range(heads):
-        if head:
+    @pl.loop(0, heads)
+    def _(head):
+        @pl.when(head > 0)
+        def _():
             send_values(head)
 
-        @pl.loop(1, n)
+        @pl.loop(1, members)
         def _(step):
-            other = peer(step)
+            other = member(step)
             cols = columns(other, head)
             sent[head, other, 0] = rotated(q_ref, gq_ref, scale_q, cols)
             sent[head, other, 1] = rotated(k_ref, gk_ref, scale_k, cols)
             remote(
-                sent.at[head, other], recv.at[head, 0:2, rows(me), :],
-                in_send.at[head], in_recv.at[head], (my_dp, other),
+                sent.at[head, other], recv.at[head, 0:2, rows(place_in), :],
+                in_send.at[head], in_recv.at[head], device(side, other),
             ).start()
 
-        cols = columns(me, head)
-        recv[head, 0, rows(me), :] = rotated(q_ref, gq_ref, scale_q, cols)
-        recv[head, 1, rows(me), :] = rotated(k_ref, gk_ref, scale_k, cols)
+        cols = columns(place_in, head)
+        for place, (ref, gain, norm) in enumerate(((q_ref, gq_ref, scale_q), (k_ref, gk_ref, scale_k))):
+            moved = rotated(ref, gain, norm, cols)
+            sent[head, place_in, place] = moved
+            recv[head, place, rows(place_in), :] = moved
+
+        def cross(group, source, target, count):
+            @pl.loop(0, members)
+            def _(step):
+                other = member(step)
+                remote(
+                    sent.at[head, other, :, source, :], recv.at[head, 0:2, target, :],
+                    cross_in_send.at[head], in_recv.at[head], device(group, other),
+                ).start()
+
+        each_crossing(cross)
 
     bounds = []
     running = len_ref[0, 0]
@@ -137,26 +187,39 @@
         if clip + 1 < clips:
             running = running + len_ref[0, clip + 1]
 
+    first, last = jnp.int32(0), jnp.int32(2 * half_tokens)
+    for bound in bounds:
+        first = jnp.maximum(first, jnp.where(bound <= half_tokens, bound, 0))
+        last = jnp.minimum(last, jnp.where(bound > half_tokens, bound, 2 * half_tokens))
+    low_owns = last - half_tokens <= half_tokens - first
+    low_edge = jnp.where(low_owns, half_tokens, first)
+    high_edge = jnp.where(low_owns, last, half_tokens)
+    tail = padded - window
+    if tail:
+        @pl.loop(0, heads)
+        def _(head):
+            recv[head, :, window:padded, :] = jnp.zeros((4, tail, HEAD_DIM), jnp.bfloat16)
+
     def segment(shape, dim, start):
-        places = lax.broadcasted_iota(jnp.int32, shape, dim) + start
+        inside = lax.broadcasted_iota(jnp.int32, shape, dim) + start
+        places = inside + side * (half_tokens - halo)
         found = jnp.zeros(shape, jnp.int32)
         for bound in bounds:
             found = found + (places >= bound).astype(jnp.int32)
-        return found
-
-    block = min(QUERY_BLOCK, tokens)
+        return jnp.where(inside < window, found, -1)
 
     @pl.loop(0, heads)
     def _(head):
-        arrived = recv.at[head, :, pl.ds(0, (n - 1) * tok), :]
+        arrived = recv.at[head, :, pl.ds(0, (members - 1) * tok + halo), :]
         pltpu.make_async_copy(arrived, arrived, in_recv.at[head]).wait()
         own = recv.at[head, pl.ds(2, 2), pl.ds(0, tok), :]
         pltpu.make_async_copy(own, own, own_sem.at[head]).wait()
         key_acc[...] = jnp.zeros_like(key_acc)
         value_acc[...] = jnp.zeros_like(value_acc)
-        for start in range(0, tokens, block):
+        for start in range(0, window, QUERY_BLOCK):
+            block = min(QUERY_BLOCK, window - start)
             low = max(0, start - reach) // LANES * LANES
-            high = min(tokens, -(-(start + block + reach) // LANES) * LANES)
+            high = min(padded, -(-(start + block + reach) // LANES) * LANES)
             query = recv[head, 0, start:start + block, :]
             keys = recv[head, 1, low:high, :]
             value_rows = recv[head, 2, low:high, :]
@@ -177,18 +240,35 @@
             back[head, 1, start:start + block, :] = dot(dscore, keys, 1, 0).astype(jnp.bfloat16)
             key_acc[low:high, :] += dot(dscore, query, 0, 0)
             value_acc[low:high, :] += dot(half, cot, 0, 0)
-        back[head, 2] = key_acc[...].astype(jnp.bfloat16)
-        back[head, 3] = value_acc[...].astype(jnp.bfloat16)
-
-        @pl.loop(1, n)
+        back[head, 2] = key_acc[0:window, :].astype(jnp.bfloat16)
+        back[head, 3] = value_acc[0:window, :].astype(jnp.bfloat16)
+        cols = columns(place_in, head)
+        for d, count in crossing:
+            @pl.when(side == 0)
+            def _():
+                edge = half_tokens + d * tok
+                remote(
+                    back.at[head, :, edge:edge + count, :], other_out.at[:, 0:count, cols],
+                    cross_out_send.at[head], cross_out_recv.at[head], device(1, d),
+                ).start()
+
+            @pl.when(side == 1)
+            def _():
+                edge = halo - d * tok - count
+                remote(
+                    back.at[head, :, edge:edge + count, :], other_out.at[:, tok - count:tok, cols],
+                    cross_out_send.at[head], cross_out_recv.at[head], device(0, members - 1 - d),
+                ).start()
+
+        @pl.loop(1, members)
         def _(step):
-            other = peer(step)
+            other = member(step)
             remote(
-                back.at[head, :, rows(other), :], out_ref.at[:, :, columns(me, head)],
-                out_send.at[head], out_recv.at[head], (my_dp, other),
+                back.at[head, :, rows(other), :], out_ref.at[:, :, cols],
+                out_send.at[head], out_recv.at[head], device(side, other),
             ).start()
 
-        out_ref[:, :, columns(me, head)] = back[head, :, rows(me), :]
+        out_ref[:, :, cols] = back[head, :, rows(place_in), :]
 
     def turned_back(place, ref, norm, cols):
         grads = out_ref[place, :, cols].astype(jnp.float32)
@@ -197,8 +277,24 @@
 
     inner = (zero, zero)
     for head in range(heads):
-        arrived = out_ref.at[:, :, pl.ds(0, (n - 1) * HEAD_DIM)]
+        arrived = out_ref.at[:, :, pl.ds(0, (members - 1) * HEAD_DIM)]
         pltpu.make_async_copy(arrived, arrived, out_recv.at[head]).wait()
+
+        def merge(group, source, target, count):
+            crossed = other_out.at[:, source, pl.ds(0, members * HEAD_DIM)]
+            pltpu.make_async_copy(crossed, crossed, cross_out_recv.at[head]).wait()
+            places = lax.broadcasted_iota(jnp.int32, (count, HEAD_DIM), 0) + me * tok + source.start
+            outside = (places >= low_edge) if group == 1 else (places < high_edge)
+
+            @pl.loop(0, members)
+            def _(owner):
+                cols = columns(owner, head)
+                for place in range(4):
+                    out_ref[place, source, cols] = jnp.where(
+                        outside, other_out[place, source, cols], out_ref[place, source, cols]
+                    )
+
+        each_crossing(merge)
 
         def first_pass(owner, sums):
             cols = columns(owner, head)
@@ -208,12 +304,12 @@
             ):
                 turned, hat = turned_back(place + 1, ref, norm, cols)
                 both = turned * hat
-                row = place * heads + head
-                part[owner, row:row + 1, :] = jnp.sum(both, axis=0, keepdims=True)
+                row = place * shared + head % shared
+                part[owner * 2 + head // shared, row:row + 1, :] = jnp.sum(both, axis=0, keepdims=True)
                 results.append(sums[place] + both * gain[:, cols])
             return tuple(results)
 
-        inner = lax.fori_loop(0, n, first_pass, inner)
+        inner = lax.fori_loop(0, members, first_pass, inner)
 
     @pl.loop(1, n)
     def _(step):
@@ -268,23 +364,35 @@
     wait_all(dp_part, replicas - 1, gain_send.at[1])
     wait_all(seq_part, n - 1, gain_send.at[2])
     for head in range(heads):
-        moved = recv.at[head, :, pl.ds(0, (n - 1) * tok), :]
+        moved = recv.at[head, :, pl.ds(0, (members - 1) * tok), :]
         pltpu.make_async_copy(moved, moved, in_send.at[head]).wait()
         pltpu.make_async_copy(moved, moved, out_send.at[head]).wait()
+        moved = recv.at[head, :, pl.ds(0, halo), :]
+        pltpu.make_async_copy(moved, moved, cross_out_send.at[head]).wait()
+
+        def drain(group, source, target, count):
+            moved = other_out.at[:, source, pl.ds(0, members * HEAD_DIM)]
+            pltpu.make_async_copy(moved, moved, cross_in_send.at[head]).wait()
+
+        each_crossing(drain)
 
 
 def on_device(q_raw, k_raw, values, grad_out, q_gain, k_gain, lengths, positions):
     n = lax.axis_size("seq")
     replicas = lax.axis_size("dp")
     tok, feature = q_raw.shape[1:]
-    heads = feature // n // HEAD_DIM
+    shared = feature // n // HEAD_DIM
+    heads = 2 * shared
     tokens = n * tok
     reach = tokens // 3 - 1
+    halo = -(-((reach + 1) // 2) // 16) * 16
+    window = tokens // 2 + halo
+    padded = -(-window // LANES) * LANES
     cosine, sine = rope_tables(positions[0], HEAD_DIM)
-    sizes = (n, replicas, heads, tok, lengths.shape[1], reach)
+    sizes = (n, replicas, heads, tok, lengths.shape[1], reach, halo, padded)
     vmem = pl.BlockSpec(memory_space=pltpu.VMEM)
     hbm = pl.BlockSpec(memory_space=pl.ANY)
-    gain_rows = (2 * heads, LANES)
+    gain_rows = (2 * shared, LANES)
     half, full = jnp.bfloat16, jnp.float32
     outs, gains = pl.pallas_call(
         functools.partial(kernel, sizes),
@@ -297,11 +405,12 @@
         ],
         out_specs=(vmem, vmem),
         scratch_shapes=[
-            pltpu.VMEM((heads, n, 2, tok, HEAD_DIM), half),
-            pltpu.VMEM((heads, 4, tokens, HEAD_DIM), half),
-            pltpu.VMEM((heads, 4, tokens, HEAD_DIM), half),
-            pltpu.VMEM((tokens, HEAD_DIM), full),
-            pltpu.VMEM((tokens, HEAD_DIM), full),
+            pltpu.VMEM((4, tok, feature), half),
+            pltpu.VMEM((heads, n // 2, 2, tok, HEAD_DIM), half),
+            pltpu.VMEM((heads, 4, padded, HEAD_DIM), half),
+            pltpu.VMEM((heads, 4, window, HEAD_DIM), half),
+            pltpu.VMEM((padded, HEAD_DIM), full),
+            pltpu.VMEM((padded, HEAD_DIM), full),
             pltpu.VMEM((tok, LANES), full),
             pltpu.VMEM((tok, LANES), full),
             pltpu.VMEM((n,) + gain_rows, full),
@@ -316,6 +425,9 @@
             pltpu.SemaphoreType.DMA((heads,)),
             pltpu.SemaphoreType.DMA((3,)),
             pltpu.SemaphoreType.DMA((3,)),
+            pltpu.SemaphoreType.DMA((heads,)),
+            pltpu.SemaphoreType.DMA((heads,)),
+            pltpu.SemaphoreType.DMA((heads,)),
         ],
         compiler_params=pltpu.CompilerParams(
             collective_id=0, has_side_effects=True, vmem_limit_bytes=56 * 1024 * 1024
@@ -324,7 +436,7 @@
         lengths, q_raw[0], k_raw[0], values[0], grad_out[0],
         q_gain[None], k_gain[None], cosine, sine,
     )
-    gains = gains.reshape(n, 2, heads * HEAD_DIM)
+    gains = gains.reshape(n, 2, shared * HEAD_DIM)
     return (
         outs[0][None], outs[1][None], outs[2][None], outs[3][None],
         gains[:, 0].reshape(feature), gains[:, 1].reshape(feature),

time: 212 us -> 189 us (0.89)
  Pallas kernels: 204 us -> 180 us
    pallas_call x1, Pallas kernels: 204 us -> 180 us  [on_device(): pl.pallas_call(functools.partial(kernel, sizes), out_shape=(jax.ShapeDtyp...]
where the time goes in v2:
time: 189 us; the launch traced here: 188 us
  Pallas kernels  180 us (95%)
  local copies, waits for them, and re-layouts  4.95 us (3%)
  other arithmetic  2.39 us (1%)
    pallas_call x1, Pallas kernels, on_device(): pl.pallas_call(functools.partial(kernel, sizes), out_shape=(jax.ShapeDtyp...  180 us
    slice x1, local copies, waits for them, and re-layouts, on_device(): outs[3][None]  4.28 us

profile of v2, /device:TPU:0, one launch (start us, length us, event | category | flops | bytes accessed | tf_op | source)
XLA Modules:
  0.0 188.4 jit_solution(7898116404419284663)
XLA Ops:
  0.6 0.7 convert_element_type.4
  1.3 1.7 sine_multiply_fusion
  3.0 180.4 %shard_map.163 = (bf16[4,128,4096]{2,1,0:T(8,128)(2,1)}, f32[8,8,128]{2,1,0:T(8,128)}) custom-call(s32[1,6]{1,0:T(1,128)} %len_ref.1, bf16[128,4096]{1,0:T(8,128)(2,1)} %bitcast.14, bf16[128,4096]{1,0:T(8,128)(2,1)} %bitcast.15, bf16[128,4096]{1,0:T(8,128)(2,1)} %bitcast.16, bf16[128,4096]{1,0:T(8,128)(2,1)} %bitcast.17, f32[1,4096]{1,0:T(1,128)} %bitcast.18, ...), custom_call_target="tpu_custom_call" | custom-call | tf_op jit(solution)/shard_map/pallas_call | solution.py:397
  183.4 0.0 copy-start
  183.4 4.3 %fusion.1 = (bf16[1,128,4096]{2,1,0:T(8,128)(2,1)}, bf16[1,128,4096]{2,1,0:T(8,128)(2,1)}, bf16[1,128,4096]{2,1,0:T(8,128)(2,1)}, bf16[1,128,4096]{2,1,0:T(8,128)(2,1)}) fusion(bf16[4,128,4096]{2,1,0:T(8,128)(2,1)} %get-tuple-element.8), kind=kLoop, calls=%fused_computation.6 | loop fusion | bytes 8388608 | tf_op jit(solution)/shard_map/slice | solution.py:441
  187.7 0.0 copy-done
  187.7 0.6 fusion.2
  (2 shorter events, 0.0 us)
Async XLA Ops:
  183.4 4.3 %copy-start = (f32[8,8,128]{2,1,0:T(8,128)S(1)}, f32[8,8,128]{2,1,0:T(8,128)}, u32[]{:S(2)}) copy-start(f32[8,8,128]{2,1,0:T(8,128)} %get-tuple-element.9) | copy-start | bytes 98308

commit v3 on v2

--- a/solution.py
+++ b/solution.py
@@ -11,6 +11,9 @@
 HEAD_DIM = 128
 LANES = 128
 QUERY_BLOCK = 256
+GROUPS = 4
+ATTEND_LAG = 2
+DISTRIBUTE_LAG = 2
 EPSILON = 1e-06
 MESH = pl.DeviceIdType.MESH
 
@@ -41,22 +44,22 @@
     sizes,
     len_ref, q_ref, k_ref, v_ref, do_ref, gq_ref, gk_ref, cos_ref, sin_ref,
     out_ref, gain_ref,
-    other_out, sent, recv, back, key_acc, value_acc, scale_q, scale_k,
+    beside, sent, recv, back, key_acc, value_acc, scale_q, scale_k,
     part, seq_part, dp_sum, dp_part, total,
     in_send, in_recv, own_sem, out_send, out_recv, gain_send, gain_recv,
-    cross_in_send, cross_out_send, cross_out_recv,
+    halo_send, halo_recv, beside_send, beside_recv,
 ):
     n, replicas, heads, tok, clips, reach, halo, padded = sizes
-    members = n // 2
-    half_tokens = members * tok
-    window = half_tokens + halo
+    members = n // GROUPS
+    group_tokens = members * tok
+    group_end = halo + group_tokens
+    window = group_end + halo
     feature = members * heads * HEAD_DIM
-    shared = heads // 2
+    ratio = GROUPS
+    shared = heads // ratio
     me = lax.axis_index("seq")
     side = me // members
     place_in = lax.rem(me, members)
-    base = side * halo
-    crossing = [(d, min(tok, halo - d * tok)) for d in range(-(-halo // tok))]
     my_dp = lax.axis_index("dp")
     scale = HEAD_DIM ** (-0.5)
 
@@ -73,17 +76,16 @@
         return pl.ds(pl.multiple_of((owner * heads + head) * HEAD_DIM, HEAD_DIM), HEAD_DIM)
 
     def rows(owner):
-        return pl.ds(pl.multiple_of(base + owner * tok, 16), tok)
-
-    def each_crossing(act):
-        for d, count in crossing:
-            @pl.when(me == members - 1 - d)
-            def _():
-                act(1, slice(tok - count, tok), slice(halo - d * tok - count, halo - d * tok), count)
-
-            @pl.when(me == members + d)
-            def _():
-                act(0, slice(0, count), slice(half_tokens + d * tok, half_tokens + d * tok + count), count)
+        return pl.ds(pl.multiple_of(halo + owner * tok, 16), tok)
+
+    def each_side(act):
+        @pl.when(side > 0)
+        def _():
+            act(0, side - 1)
+
+        @pl.when(side < GROUPS - 1)
+        def _():
+            act(1, side + 1)
 
     def remote(src, dst, send_sem, recv_sem, device):
         return pltpu.make_async_remote_copy(
@@ -105,18 +107,6 @@
             pltpu.make_async_copy(
                 ref.at[:, cols], recv.at[head, place, rows(place_in), :], own_sem.at[head]
             ).start()
-
-        def cross(group, source, target, count):
-            @pl.loop(0, members)
-            def _(step):
-                other = member(step)
-                for place, ref in ((2, v_ref), (3, do_ref)):
-                    remote(
-                        ref.at[source, columns(other, head)], recv.at[head, place, target, :],
-                        cross_in_send.at[head], in_recv.at[head], device(group, other),
-                    ).start()
-
-        each_crossing(cross)
 
         @pl.loop(1, members)
         def _(step):
@@ -165,20 +155,7 @@
 
         cols = columns(place_in, head)
         for place, (ref, gain, norm) in enumerate(((q_ref, gq_ref, scale_q), (k_ref, gk_ref, scale_k))):
-            moved = rotated(ref, gain, norm, cols)
-            sent[head, place_in, place] = moved
-            recv[head, place, rows(place_in), :] = moved
-
-        def cross(group, source, target, count):
-            @pl.loop(0, members)
-            def _(step):
-                other = member(step)
-                remote(
-                    sent.at[head, other, :, source, :], recv.at[head, 0:2, target, :],
-                    cross_in_send.at[head], in_recv.at[head], device(group, other),
-                ).start()
-
-        each_crossing(cross)
+            recv[head, place, rows(place_in), :] = rotated(ref, gain, norm, cols)
 
     bounds = []
     running = len_ref[0, 0]
@@ -187,33 +164,68 @@
         if clip + 1 < clips:
             running = running + len_ref[0, clip + 1]
 
-    first, last = jnp.int32(0), jnp.int32(2 * half_tokens)
-    for bound in bounds:
-        first = jnp.maximum(first, jnp.where(bound <= half_tokens, bound, 0))
-        last = jnp.minimum(last, jnp.where(bound > half_tokens, bound, 2 * half_tokens))
-    low_owns = last - half_tokens <= half_tokens - first
-    low_edge = jnp.where(low_owns, half_tokens, first)
-    high_edge = jnp.where(low_owns, last, half_tokens)
-    tail = padded - window
-    if tail:
+    def edges(middle):
+        first, last = jnp.int32(0), jnp.int32(n * tok)
+        for bound in bounds:
+            first = jnp.maximum(first, jnp.where(bound <= middle, bound, 0))
+            last = jnp.minimum(last, jnp.where(bound > middle, bound, n * tok))
+        low_owns = last - middle <= middle - first
+        return jnp.where(low_owns, middle, first), jnp.where(low_owns, last, middle)
+
+    token_start = side * group_tokens
+    high_edge = edges(token_start)[1]
+    low_edge = edges(token_start + group_tokens)[0]
+
+    def clear(begin, end):
         @pl.loop(0, heads)
         def _(head):
-            recv[head, :, window:padded, :] = jnp.zeros((4, tail, HEAD_DIM), jnp.bfloat16)
+            recv[head, :, begin:end, :] = jnp.zeros((4, end - begin, HEAD_DIM), jnp.bfloat16)
+
+    if padded > window:
+        clear(window, padded)
+
+    @pl.when(side == 0)
+    def _():
+        clear(0, halo)
+
+    @pl.when(side == GROUPS - 1)
+    def _():
+        clear(group_end, window)
 
     def segment(shape, dim, start):
         inside = lax.broadcasted_iota(jnp.int32, shape, dim) + start
-        places = inside + side * (half_tokens - halo)
+        places = inside + (token_start - halo)
         found = jnp.zeros(shape, jnp.int32)
         for bound in bounds:
             found = found + (places >= bound).astype(jnp.int32)
-        return jnp.where(inside < window, found, -1)
-
-    @pl.loop(0, heads)
-    def _(head):
-        arrived = recv.at[head, :, pl.ds(0, (members - 1) * tok + halo), :]
+        valid = (inside < window) & (places >= 0) & (places < n * tok)
+        return jnp.where(valid, found, -1)
+
+    group_rows = ((halo, halo + halo), (group_end - halo, group_end))
+    halo_rows = ((0, halo), (group_end, window))
+
+    def relay(head):
+        arrived = recv.at[head, :, pl.ds(0, (members - 1) * tok), :]
         pltpu.make_async_copy(arrived, arrived, in_recv.at[head]).wait()
         own = recv.at[head, pl.ds(2, 2), pl.ds(0, tok), :]
         pltpu.make_async_copy(own, own, own_sem.at[head]).wait()
+
+        def act(which, group):
+            source, target = group_rows[which], halo_rows[1 - which]
+            remote(
+                recv.at[head, :, source[0]:source[1], :], recv.at[head, :, target[0]:target[1], :],
+                halo_send.at[which, head], halo_recv.at[1 - which, head], device(group, place_in),
+            ).start()
+
+        each_side(act)
+
+    def attend(head):
+        def arrive(which, group):
+            target = halo_rows[which]
+            held = recv.at[head, :, target[0]:target[1], :]
+            pltpu.make_async_copy(held, held, halo_recv.at[which, head]).wait()
+
+        each_side(arrive)
         key_acc[...] = jnp.zeros_like(key_acc)
         value_acc[...] = jnp.zeros_like(value_acc)
         for start in range(0, window, QUERY_BLOCK):
@@ -242,23 +254,33 @@
             value_acc[low:high, :] += dot(half, cot, 0, 0)
         back[head, 2] = key_acc[0:window, :].astype(jnp.bfloat16)
         back[head, 3] = value_acc[0:window, :].astype(jnp.bfloat16)
+
+        def act(which, group):
+            source = halo_rows[which]
+            remote(
+                back.at[head, :, source[0]:source[1], :], beside.at[head, 1 - which],
+                beside_send.at[which, head], beside_recv.at[1 - which, head],
+                device(group, place_in),
+            ).start()
+
+        each_side(act)
+
+    def distribute(head):
+        def merge(which, group):
+            held = beside.at[head, which]
+            pltpu.make_async_copy(held, held, beside_recv.at[which, head]).wait()
+            begin, end = group_rows[which]
+            places = lax.broadcasted_iota(jnp.int32, (halo, HEAD_DIM), 0) + (
+                token_start + begin - halo
+            )
+            outside = (places >= low_edge) if which else (places < high_edge)
+            for place in range(4):
+                back[head, place, begin:end, :] = jnp.where(
+                    outside, beside[head, which, place], back[head, place, begin:end, :]
+                )
+
+        each_side(merge)
         cols = columns(place_in, head)
-        for d, count in crossing:
-            @pl.when(side == 0)
-            def _():
-                edge = half_tokens + d * tok
-                remote(
-                    back.at[head, :, edge:edge + count, :], other_out.at[:, 0:count, cols],
-                    cross_out_send.at[head], cross_out_recv.at[head], device(1, d),
-                ).start()
-
-            @pl.when(side == 1)
-            def _():
-                edge = halo - d * tok - count
-                remote(
-                    back.at[head, :, edge:edge + count, :], other_out.at[:, tok - count:tok, cols],
-                    cross_out_send.at[head], cross_out_recv.at[head], device(0, members - 1 - d),
-                ).start()
 
         @pl.loop(1, members)
         def _(step):
@@ -270,6 +292,20 @@
 
         out_ref[:, :, cols] = back[head, :, rows(place_in), :]
 
+    @pl.loop(0, heads + ATTEND_LAG + DISTRIBUTE_LAG)
+    def _(step):
+        @pl.when(step < heads)
+        def _():
+            relay(step)
+
+        @pl.when((step >= ATTEND_LAG) & (step < heads + ATTEND_LAG))
+        def _():
+            attend(step - ATTEND_LAG)
+
+        @pl.when(step >= ATTEND_LAG + DISTRIBUTE_LAG)
+        def _():
+            distribute(step - ATTEND_LAG - DISTRIBUTE_LAG)
+
     def turned_back(place, ref, norm, cols):
         grads = out_ref[place, :, cols].astype(jnp.float32)
         turned = grads * cos_ref[...] - pltpu.roll(grads, HEAD_DIM // 2, 1) * sin_ref[...]
@@ -279,22 +315,6 @@
     for head in range(heads):
         arrived = out_ref.at[:, :, pl.ds(0, (members - 1) * HEAD_DIM)]
         pltpu.make_async_copy(arrived, arrived, out_recv.at[head]).wait()
-
-        def merge(group, source, target, count):
-            crossed = other_out.at[:, source, pl.ds(0, members * HEAD_DIM)]
-            pltpu.make_async_copy(crossed, crossed, cross_out_recv.at[head]).wait()
-            places = lax.broadcasted_iota(jnp.int32, (count, HEAD_DIM), 0) + me * tok + source.start
-            outside = (places >= low_edge) if group == 1 else (places < high_edge)
-
-            @pl.loop(0, members)
-            def _(owner):
-                cols = columns(owner, head)
-                for place in range(4):
-                    out_ref[place, source, cols] = jnp.where(
-                        outside, other_out[place, source, cols], out_ref[place, source, cols]
-                    )
-
-        each_crossing(merge)
 
         def first_pass(owner, sums):
             cols = columns(owner, head)
@@ -305,7 +325,7 @@
                 turned, hat = turned_back(place + 1, ref, norm, cols)
                 both = turned * hat
                 row = place * shared + head % shared
-                part[owner * 2 + head // shared, row:row + 1, :] = jnp.sum(both, axis=0, keepdims=True)
+                part[owner * ratio + head // shared, row:row + 1, :] = jnp.sum(both, axis=0, keepdims=True)
                 results.append(sums[place] + both * gain[:, cols])
             return tuple(results)
 
@@ -367,14 +387,13 @@
         moved = recv.at[head, :, pl.ds(0, (members - 1) * tok), :]
         pltpu.make_async_copy(moved, moved, in_send.at[head]).wait()
         pltpu.make_async_copy(moved, moved, out_send.at[head]).wait()
-        moved = recv.at[head, :, pl.ds(0, halo), :]
-        pltpu.make_async_copy(moved, moved, cross_out_send.at[head]).wait()
-
-        def drain(group, source, target, count):
-            moved = other_out.at[:, source, pl.ds(0, members * HEAD_DIM)]
-            pltpu.make_async_copy(moved, moved, cross_in_send.at[head]).wait()
-
-        each_crossing(drain)
+
+        def drain(which, group):
+            held = beside.at[head, which]
+            pltpu.make_async_copy(held, held, halo_send.at[which, head]).wait()
+            pltpu.make_async_copy(held, held, beside_send.at[which, head]).wait()
+
+        each_side(drain)
 
 
 def on_device(q_raw, k_raw, values, grad_out, q_gain, k_gain, lengths, positions):
@@ -382,11 +401,11 @@
     replicas = lax.axis_size("dp")
     tok, feature = q_raw.shape[1:]
     shared = feature // n // HEAD_DIM
-    heads = 2 * shared
+    heads = GROUPS * shared
     tokens = n * tok
     reach = tokens // 3 - 1
     halo = -(-((reach + 1) // 2) // 16) * 16
-    window = tokens // 2 + halo
+    window = tokens // GROUPS + 2 * halo
     padded = -(-window // LANES) * LANES
     cosine, sine = rope_tables(positions[0], HEAD_DIM)
     sizes = (n, replicas, heads, tok, lengths.shape[1], reach, halo, padded)
@@ -405,8 +424,8 @@
         ],
         out_specs=(vmem, vmem),
         scratch_shapes=[
-            pltpu.VMEM((4, tok, feature), half),
-            pltpu.VMEM((heads, n // 2, 2, tok, HEAD_DIM), half),
+            pltpu.VMEM((heads, 2, 4, halo, HEAD_DIM), half),
+            pltpu.VMEM((heads, n // GROUPS, 2, tok, HEAD_DIM), half),
             pltpu.VMEM((heads, 4, padded, HEAD_DIM), half),
             pltpu.VMEM((heads, 4, window, HEAD_DIM), half),
             pltpu.VMEM((padded, HEAD_DIM), full),
@@ -425,9 +444,10 @@
             pltpu.SemaphoreType.DMA((heads,)),
             pltpu.SemaphoreType.DMA((3,)),
             pltpu.SemaphoreType.DMA((3,)),
-            pltpu.SemaphoreType.DMA((heads,)),
-            pltpu.SemaphoreType.DMA((heads,)),
-            pltpu.SemaphoreType.DMA((heads,)),
+            pltpu.SemaphoreType.DMA((2, heads)),
+            pltpu.SemaphoreType.DMA((2, heads)),
+            pltpu.SemaphoreType.DMA((2, heads)),
+            pltpu.SemaphoreType.DMA((2, heads)),
         ],
         compiler_params=pltpu.CompilerParams(
             collective_id=0, has_side_effects=True, vmem_limit_bytes=56 * 1024 * 1024

time: 189 us -> 165 us (0.87)
  Pallas kernels: 180 us -> 157 us
    pallas_call x1, Pallas kernels: 180 us -> 157 us  [on_device(): pl.pallas_call(functools.partial(kernel, sizes), out_shape=(jax.ShapeDtyp...]
where the time goes in v3:
time: 165 us
  Pallas kernels  157 us (95%)
  local copies, waits for them, and re-layouts  4.95 us (3%)
  other arithmetic  2.39 us (1%)
    pallas_call x1, Pallas kernels, on_device(): pl.pallas_call(functools.partial(kernel, sizes), out_shape=(jax.ShapeDtyp...  157 us
    slice x1, local copies, waits for them, and re-layouts, on_device(): outs[3][None]  4.28 us

profile of v3, /device:TPU:0, one launch (start us, length us, event | category | flops | bytes accessed | tf_op | source)
XLA Modules:
  0.0 165.2 jit_solution(5898242274357154930)
XLA Ops:
  0.6 0.7 convert_element_type.4
  1.3 1.7 %sine_multiply_fusion = (f32[128,128]{1,0:T(8,128)}, f32[128,128]{1,0:T(8,128)}) fusion(f32[128]{0:T(128)} %constant.11.clone, f32[128]{0:T(128)} %constant.10.clone, f32[128]{0:T(128)S(1)} %get-tuple-element.19, f32[128]{0:T(128)S(1)} %get-tuple-element.20, f32[128]{0:T(128)S(1)} %get-tuple-element.18, pred[128]{0:T(512)(128)(4,1)} %constant.8.clone, ...), kind=kLoop, calls=%fused_computation | loop fusion | flops 65536 | bytes 133888 | tf_op jit(solution)/shard_map/mul | solution.py:34
  3.0 157.2 %shard_map.163 = (bf16[4,128,4096]{2,1,0:T(8,128)(2,1)}, f32[8,8,128]{2,1,0:T(8,128)}) custom-call(s32[1,6]{1,0:T(1,128)} %len_ref.1, bf16[128,4096]{1,0:T(8,128)(2,1)} %bitcast.14, bf16[128,4096]{1,0:T(8,128)(2,1)} %bitcast.15, bf16[128,4096]{1,0:T(8,128)(2,1)} %bitcast.16, bf16[128,4096]{1,0:T(8,128)(2,1)} %bitcast.17, f32[1,4096]{1,0:T(1,128)} %bitcast.18, ...), custom_call_target="tpu_custom_call" | custom-call | tf_op jit(solution)/shard_map/pallas_call | solution.py:416
  160.3 0.0 copy-start
  160.3 4.3 %fusion.1 = (bf16[1,128,4096]{2,1,0:T(8,128)(2,1)}, bf16[1,128,4096]{2,1,0:T(8,128)(2,1)}, bf16[1,128,4096]{2,1,0:T(8,128)(2,1)}, bf16[1,128,4096]{2,1,0:T(8,128)(2,1)}) fusion(bf16[4,128,4096]{2,1,0:T(8,128)(2,1)} %get-tuple-element.8), kind=kLoop, calls=%fused_computation.6 | loop fusion | bytes 8388608 | tf_op jit(solution)/shard_map/slice | solution.py:461
  164.6 0.0 copy-done
  164.6 0.6 fusion.2
  (2 shorter events, 0.0 us)
Async XLA Ops:
  160.3 4.3 %copy-start = (f32[8,8,128]{2,1,0:T(8,128)S(1)}, f32[8,8,128]{2,1,0:T(8,128)}, u32[]{:S(2)}) copy-start(f32[8,8,128]{2,1,0:T(8,128)} %get-tuple-element.9) | copy-start | bytes 98308
